TPU v7x, 512 devices: a whole 4x8x8 slice. The times are simulated.
512 devices in a mesh: seq: 32 (over y, x), trow: 2 (over core), tcol: 8 (over z).
Axes of the slice: x: 4, y: 8, z: 8, core: 2. Of those that a mesh axis runs over, the one named last changes fastest.
Arguments:
- tokens: bfloat16 [16384, 4096], P('seq', ('trow', 'tcol')), may hold values from -24 to 24
- norm_gain: float32 [4096], replicated, may hold values from 0.1 to 1.9
- in_weight: bfloat16 [3, 4096, 8192], P(None, None, ('trow', 'tcol')), may hold values from -0.09375 to 0.09375
- filter_taps: float32 [128, 8192], P(None, ('trow', 'tcol')), may hold values from -0.5 to 0.5
- conv_skip: float32 [8192], P(('trow', 'tcol')), may hold values from -1 to 1
- out_weight: bfloat16 [8192, 4096], P(('trow', 'tcol')), may hold values from -0.09375 to 0.09375
Outputs:
- mixer_out: bfloat16 [16384, 4096], P('seq', ('trow', 'tcol'))
All inputs are finite; a program needn't handle non-finite values.
Results may differ from a plain program's by a relative error of at most 0.03.
Values may be sent and summed in bfloat16 or wider, within the bound.
A program may use at most 64 MiB of HBM per device.

v0:
```python
import jax
import jax.numpy as jnp
from jax import lax
from jax.sharding import PartitionSpec as P


def passed_along(block, axis, distance):
    devices = range(lax.axis_size(axis))
    route = [(i - distance, i) for i in devices if i - distance in devices]
    return lax.ppermute(block, axis, route)


def on_device(tokens, norm_gain, in_weight, filter_taps, conv_skip, out_weight):
    whole = lax.all_gather(tokens, ("trow", "tcol"), axis=1, tiled=True)
    wide = whole.astype(jnp.float32)
    mean_square = jnp.mean(wide * wide, axis=1, keepdims=True)
    normed = (wide * lax.rsqrt(mean_square + 1e-06) * norm_gain).astype(jnp.bfloat16)
    query = jnp.dot(normed, in_weight[0], preferred_element_type=jnp.float32).astype(jnp.bfloat16)
    keys = jnp.dot(normed, in_weight[1], preferred_element_type=jnp.float32).astype(jnp.bfloat16)
    values = jnp.dot(normed, in_weight[2], preferred_element_type=jnp.float32).astype(jnp.bfloat16)
    mixed = (keys.astype(jnp.float32) * values.astype(jnp.float32)).astype(jnp.bfloat16)
    taps = filter_taps.shape[0]
    rows = mixed.shape[0]
    channels = mixed.shape[1]
    tail_rows = mixed[rows - (taps - 1) :]
    previous = passed_along(tail_rows, "seq", 1)
    extended = jnp.concatenate([previous, mixed], axis=0)

    def tap_group(group, total):
        for inner in range(8):
            index = group * 8 + inner
            window = lax.dynamic_slice_in_dim(extended, taps - 1 - index, rows, 0)
            weight = lax.dynamic_slice_in_dim(filter_taps, index, 1, 0)
            total = total + window.astype(jnp.float32) * weight
        return total

    filtered = lax.fori_loop(0, taps // 8, tap_group, jnp.zeros((rows, channels), jnp.float32))
    filtered = filtered + conv_skip * mixed.astype(jnp.float32)
    gated = (query.astype(jnp.float32) * filtered).astype(jnp.bfloat16)
    partial_sum = jnp.dot(gated, out_weight, preferred_element_type=jnp.float32)
    summed = lax.psum_scatter(
        partial_sum.astype(jnp.bfloat16), ("trow", "tcol"), scatter_dimension=1, tiled=True
    )
    return summed


def solution(mesh):
    placed = (
        P("seq", ("trow", "tcol")),
        P(),
        P(None, None, ("trow", "tcol")),
        P(None, ("trow", "tcol")),
        P(("trow", "tcol")),
        P(("trow", "tcol"), None),
    )
    return jax.shard_map(
        on_device, mesh=mesh, in_specs=placed, out_specs=P("seq", ("trow", "tcol")), check_vma=False
    )
```

profile of v0, /device:TPU:1, one launch (start us, length us, event | category | flops | bytes accessed | tf_op | source)
XLA Modules:
  0.0 220.7 jit_solution(7478278523960679927)
XLA Ops:
  7.3 59.9 %all-gather.2.cloned.1.call-done = bf16[512,4096]{1,0:T(8,128)(2,1)} async-done(((bf16[512,256]{1,0:T(8,128)(2,1)}), bf16[512,4096]{1,0:T(8,128)(2,1)}) %all-gather.2.cloned.1.call-update) | async-done | bytes 4194320 | tf_op jit(solution)/shard_map/all_gather | solution.py:14
  67.2 3.2 %fusion.7 = f32[512]{0:T(512)S(1)} fusion(bf16[512,4096]{1,0:T(8,128)(2,1)} %all-gather.2.cloned.1.call-done), kind=kLoop, calls=%fused_computation.18 | loop fusion | flops 6290944 | bytes 4196352 | tf_op jit(solution)/shard_map/reduce_sum | solution.py:16
  70.6 4.6 %fusion.46 = f32[512,512]{1,0:T(8,128)S(1)} fusion(bf16[3,4096,512]{2,1,0:T(8,128)(2,1)} %param.10, bf16[512,4096]{1,0:T(8,128)(2,1)S(1)} %copy-done, f32[4096]{0:T(1024)S(1)} %copy-done.1, f32[512]{0:T(512)S(1)} %add_rsqrt_fusion), kind=kOutput, calls=%fused_computation.40 | convolution fusion | flops 2156396544 | bytes 9455616 | tf_op jit(solution)/shard_map/dot_general | solution.py:20
  75.2 4.6 %fusion.40 = bf16[512,512]{1,0:T(8,128)(2,1)S(1)} fusion(f32[512,512]{1,0:T(8,128)S(1)} %fusion.46, bf16[3,4096,512]{2,1,0:T(8,128)(2,1)} %param.10, bf16[512,4096]{1,0:T(8,128)(2,1)S(1)} %copy-done, f32[4096]{0:T(1024)S(1)} %copy-done.1, f32[512]{0:T(512)S(1)} %add_rsqrt_fusion), kind=kOutput, calls=%fused_computation.38 | convolution fusion | flops 2156920832 | bytes 9979904 | tf_op jit(solution)/shard_map/dot_general | solution.py:19
  79.8 3.1 %collective-permute-start = (bf16[127,512]{1,0:T(8,128)(2,1)S(1)}, bf16[127,512]{1,0:T(8,128)(2,1)S(1)}, u32[]{:S(2)}, u32[]{:S(2)}) collective-permute-start(bf16[127,512]{1,0:T(8,128)(2,1)S(1)} %slice.16), channel_id=1, source_target_pairs={{0,16},{16,32},{32,48},{48,64},{64,80},{80,96},{96,112},{112,128},... | collective-permute-start | bytes 390152 | tf_op jit(solution)/shard_map/ppermute | solution.py:10
  82.9 2.6 %collective-permute-done = bf16[127,512]{1,0:T(8,128)(2,1)S(1)} collective-permute-done((bf16[127,512]{1,0:T(8,128)(2,1)S(1)}, bf16[127,512]{1,0:T(8,128)(2,1)S(1)}, u32[]{:S(2)}, u32[]{:S(2)}) %collective-permute-start) | collective-permute-done | bytes 130080 | tf_op jit(solution)/shard_map/ppermute | solution.py:10
  85.6 39.9 %while.17 = (s32[]{:T(128)}, f32[512,512]{1,0:T(8,128)S(1)}, bf16[639,512]{1,0:T(8,128)(2,1)S(1)}, f32[128,512]{1,0:T(8,128)}, s32[]{:T(128)}, /*index=5*/s32[]{...) while((s32[]{:T(128)}, f32[512,512]{1,0:T(8,128)S(1)}, ...), condition=%wide.region_2.0_spmd.clone, body=%wide.region_1.0_spmd.clone.sunk | while | flops 6553667 | bytes 6341631 | solution.py:37
  86.8 1.4 fusion.58
  89.3 1.3 fusion.58
  91.8 1.4 fusion.58
  94.3 1.3 fusion.58
  96.8 1.4 fusion.58
  101.7 1.4 fusion.58
  104.2 1.3 fusion.58
  106.7 1.4 fusion.58
  109.2 1.3 fusion.58
  111.7 1.4 fusion.58
  114.2 1.3 fusion.58
  116.7 1.4 fusion.58
  119.2 1.3 fusion.58
  121.7 1.4 fusion.58
  124.2 1.3 fusion.58
  125.5 11.2 %convolution_convert_fusion = bf16[512,4096]{1,0:T(8,128)(2,1)} fusion(bf16[512,4096]{1,0:T(8,128)(2,1)} %param.13, bf16[3,4096,512]{2,1,0:T(8,128)(2,1)} %param.10, f32[512,512]{1,0:T(8,128)S(1)} %get-tuple-element.156, bf16[512,512]{1,0:T(8,128)(2,1)S(1)} %fusion.40, f32[512]{0:T(512)S(1)} %copy-done.2, ...), kind=kOutput, calls=%fused_computation.21 | convolution fusion | flops 4307288064 | bytes 18370560 | tf_op jit(solution)/shard_map/dot_general | solution.py:40
  136.8 77.0 %reduce-scatter.2.cloned.1.call-done = bf16[512,256]{1,0:T(8,128)(2,1)} async-done(((bf16[512,4096]{1,0:T(8,128)(2,1)}), bf16[512,256]{1,0:T(8,128)(2,1)}) %reduce-scatter.2.cloned.1.call-update) | async-done | bytes 262160 | tf_op jit(solution)/shard_map/reduce_scatter | solution.py:41
  (31 shorter events, 19.1 us)
Async XLA Ops:
  6.5 63.9 %copy-start.1 = (f32[4096]{0:T(1024)S(1)}, f32[4096]{0:T(1024)}, u32[]{:S(2)}) copy-start(f32[4096]{0:T(1024)} %param.9) | copy-start | bytes 49156
  6.5 60.6 %all-gather.2.cloned.1.call-start = ((), (), s32[]{:S(2)}) async-start(), calls=%async_computation.1 | async-start | bytes 4456448 | tf_op jit(solution)/shard_map/all_gather | solution.py:14
  7.3 206.6 %reduce-scatter.2.cloned.1.call-start = ((), (), s32[]{:S(2)}) async-start(), calls=%async_computation.2 | async-start | bytes 4456448 | tf_op jit(solution)/shard_map/reduce_scatter | solution.py:41
  67.2 3.4 %copy-start = (bf16[512,4096]{1,0:T(8,128)(2,1)S(1)}, bf16[512,4096]{1,0:T(8,128)(2,1)}, u32[]{:S(2)}) copy-start(bf16[512,4096]{1,0:T(8,128)(2,1)} %all-gather.2.cloned.1.call-done) | copy-start | bytes 12582916
  79.8 5.7 %collective-permute-start = (bf16[127,512]{1,0:T(8,128)(2,1)S(1)}, bf16[127,512]{1,0:T(8,128)(2,1)S(1)}, u32[]{:S(2)}, u32[]{:S(2)}) collective-permute-start(bf16[127,512]{1,0:T(8,128)(2,1)S(1)} %slice.16), channel_id=1, source_target_pairs={{0,16},{16,32},{32,48},{48,64},{64,80},{80,96},{96,112},{112,128},... | collective-permute-start | bytes 390152 | tf_op jit(solution)/shard_map/ppermute | solution.py:10
  85.6 39.9 %copy-start.2 = (f32[512]{0:T(512)S(1)}, f32[512]{0:T(512)}, u32[]{:S(2)}) copy-start(f32[512]{0:T(512)} %param.12) | copy-start | bytes 6148
Sparse Core Ops, SparseCore 0:
  9.4 57.7 all-gather.1
  136.9 76.8 reduce-scatter.1
where the time goes:
time: 222 us; the launch traced here: 221 us
  waiting for transfers between devices  140 us (63%)
  other arithmetic  25 us (11%)
  matrix products  20.4 us (9%)
  local copies, waits for them, and re-layouts  16.9 us (8%)
  between operations  13.5 us (6%)
  starting transfers between devices  3.13 us (1%)
    reduce_scatter x1, waiting for transfers between devices, on_device(): lax.psum_scatter(partial_sum.astype(jnp.bfloat16), ('trow', 'tcol'), scat...  77 us
    all_gather x1, waiting for transfers between devices, on_device(): whole = lax.all_gather(tokens, ('trow', 'tcol'), axis=1, tiled=True)  59.9 us
    add x16, other arithmetic, tap_group(): total = total + window.astype(jnp.float32) * weight  21.6 us
    dynamic_slice x16, local copies, waits for them, and re-layouts, tap_group(): weight = lax.dynamic_slice_in_dim(filter_taps, index, 1, 0)  16.6 us
    dot_general x1, matrix products, on_device(): partial_sum = jnp.dot(gated, out_weight, preferred_element_type=jnp.float32)  11.2 us
    dot_general x1, matrix products, on_device(): jnp.dot(normed, in_weight[1], preferred_element_type=jnp.float32)  4.58 us
    dot_general x1, matrix products, on_device(): jnp.dot(normed, in_weight[2], preferred_element_type=jnp.float32)  4.56 us
  transfers between devices with their start and end apart: 3, of which 3 were waited for; matrix products, arithmetic and copies ran while one was open for 0% of the time, Pallas kernels for 0%

commit v1 on v0

v1 whole, which is shorter than its diff:
```python
import jax
import jax.numpy as jnp
from jax import lax
from jax.experimental import pallas as pl
from jax.experimental.pallas import tpu as pltpu
from jax.sharding import PartitionSpec as P

F32 = jnp.float32
BF16 = jnp.bfloat16
MESH = pl.DeviceIdType.MESH
EPS = 1e-06

RING = 8
ROWS = 512
HALF = 256
BLK = 256
CH = 512
TAPS = 128
PIECE = 128


def mixer_kernel(
    x_ref, gain_ref, win, taps, skip_ref, wout, out_ref,
    xg, xs, wv, wo, acc, sq, mx, tapc, gp, gbuf, hsend, hrecv, pbuf, rr, rl, sr, sl,
    right_sem, left_sem, peer_sem, got, w_sem, tap_sem, wo_sem, wo_send, wo_got,
    g_send, g_got, h_send, h_got, rr_send, rl_send, rr_got, rl_got,
):
    seq = lax.axis_index("seq")
    n_seq = lax.axis_size("seq")
    core = lax.axis_index("trow")
    z = lax.axis_index("tcol")
    other = 1 - core
    right = {"tcol": lax.rem(z + 1, RING)}
    left = {"tcol": lax.rem(z + RING - 1, RING)}
    peer = {"trow": other}
    after = {"seq": lax.rem(seq + 1, n_seq)}
    before = {"seq": lax.rem(seq + n_seq - 1, n_seq)}

    def block(on, shift):
        return on * RING + lax.rem(z + shift + RING, RING)

    slots = [(block(core, 0), block(other, 0))]
    for s in (1, 2, 3):
        slots.append((block(core, -s), block(core, s)))
        slots.append((block(other, -s), block(other, s)))
    slots.append((block(core, 4), block(other, 4)))

    def start_of(index, size):
        return pl.multiple_of(index * size, size)

    def w_copy(pair, q):
        return pltpu.make_async_copy(
            win.at[:, pl.ds(start_of(slots[pair][q], BLK), BLK), :],
            wv.at[pair, :, pl.ds(q * BLK, BLK), :],
            w_sem.at[pair, q],
        )

    def tap_copy(cb):
        return pltpu.make_async_copy(taps.at[:, pl.ds(cb * 128, 128)], tapc.at[cb], tap_sem.at[cb])

    def wo_copy(d):
        return pltpu.make_async_copy(
            wout.at[:, pl.ds(start_of(block(core, d), BLK), BLK)],
            wo.at[d, pl.ds(0, CH), :],
            wo_sem.at[d],
        )

    def remote(src, dst, send, recv, to):
        return pltpu.make_async_remote_copy(
            src_ref=src, dst_ref=dst, send_sem=send, recv_sem=recv, device_id=to, device_id_type=MESH
        )

    def wo_remote(d):
        return remote(
            wout.at[:, pl.ds(start_of(block(other, d), BLK), BLK)],
            wo.at[d, pl.ds(CH, CH), :],
            wo_send.at[d], wo_got.at[d], peer,
        )

    barrier = pltpu.get_barrier_semaphore()
    for to in (right, left, peer, after, before):
        pl.semaphore_signal(barrier, inc=1, device_id=to, device_id_type=MESH)
    for q in range(2):
        w_copy(0, q).start()
    pl.semaphore_wait(barrier, 5)

    rows_of = (pl.ds(HALF, HALF), pl.ds(0, HALF))

    def slot(h, pair, q):
        return xg.at[h, pair, :, pl.ds(q * BLK, BLK)]

    def to_right(h, s):
        src = x_ref.at[rows_of[h]] if s == 0 else slot(h, 2 * s - 1, 0)
        dst_pair, dst_q = (2 * s + 1, 0) if s < 3 else (7, 0)
        return remote(src, slot(h, dst_pair, dst_q), right_sem.at[h, s], got.at[h, dst_pair, dst_q], right)

    def to_left(h, s):
        src = x_ref.at[rows_of[h]] if s == 0 else slot(h, 2 * s - 1, 1)
        dst_pair, dst_q = (2 * s + 1, 1) if s < 3 else (7, 0)
        return remote(src, slot(h, dst_pair, dst_q), left_sem.at[h, s], got.at[h, dst_pair, dst_q], left)

    def to_peer(h, s):
        if s == 0:
            return remote(x_ref.at[rows_of[h]], slot(h, 0, 1), peer_sem.at[h, 0], got.at[h, 0, 1], peer)
        if s == 4:
            return remote(slot(h, 7, 0), slot(h, 7, 1), peer_sem.at[h, 4], got.at[h, 7, 1], peer)
        return remote(xg.at[h, 2 * s - 1], xg.at[h, 2 * s], peer_sem.at[h, s], got.at[h, 2 * s, 0], peer)

    def open_half(h):
        to_right(h, 0).start()
        to_left(h, 0).start()
        to_peer(h, 0).start()

    def arrivals(h, s):
        if s < 4:
            to_right(h, s - 1).wait_recv()
            if s < 3 or h == 0:
                to_right(h, s).start()
            to_left(h, s - 1).wait_recv()
            if s < 3 or h == 1:
                to_left(h, s).start()
        elif h == 0:
            to_right(h, 3).wait_recv()
        else:
            to_left(h, 3).wait_recv()
        to_peer(h, s).start()

    def project(h, pair):
        if h == 0:
            w_copy(pair, 0).wait()
            w_copy(pair, 1).wait()
        if pair == 0:
            xg[h, 0, :, 0:BLK] = x_ref[rows_of[h]]
            to_peer(h, 0).wait_recv()
        elif pair == 7:
            to_peer(h, 4).wait_recv()
        elif pair % 2 == 0:
            to_peer(h, pair // 2).wait_recv()

        @pl.loop(0, HALF // 32)
        def _(n):
            rows = pl.ds(pl.multiple_of(n * 32, 32), 32)
            wide = xg[h, pair, rows, :].astype(F32)
            xs[rows, :] = (wide * gp[pair : pair + 1, :]).astype(BF16)
            square = wide * wide
            square = square[:, 0:128] + square[:, 128:256] + square[:, 256:384] + square[:, 384:512]
            if pair == 0:
                sq[h, rows, :] = square
            else:
                sq[h, rows, :] += square

        @pl.loop(0, 3)
        def _(e):
            product = jnp.dot(xs[...], wv[pair, e], preferred_element_type=F32)
            if pair == 0:
                acc[e, rows_of[h], :] = product
            else:
                acc[e, rows_of[h], :] += product

    def close_half(h):
        base = HALF * (1 - h)

        @pl.loop(0, HALF // 64)
        def _(n):
            first = pl.multiple_of(base + n * 64, 64)
            rows = pl.ds(first, 64)
            total = jnp.sum(sq[h, pl.ds(pl.multiple_of(n * 64, 64), 64), :], axis=1, keepdims=True)
            scale = lax.rsqrt(total * (1.0 / (16 * BLK)) + EPS)
            keys = (acc[1, rows, :] * scale).astype(BF16).astype(F32)
            values = (acc[2, rows, :] * scale).astype(BF16).astype(F32)
            mixed = (keys * values).astype(BF16)
            acc[0, rows, :] = (acc[0, rows, :] * scale).astype(BF16).astype(F32)
            wide = mixed.astype(F32)
            for cb in range(4):
                mx[cb, pl.ds(pl.multiple_of(first + 128, 64), 64), :] = wide[:, cb * 128 : cb * 128 + 128]
            if h == 0:
                hsend[pl.ds(pl.multiple_of(n * 64, 64), 64), :] = mixed

    def halo():
        return remote(hsend.at[pl.ds(128, 128)], hrecv, h_send.at[0], h_got.at[0], after)

    def take_halo():
        halo().wait_recv()
        wide = jnp.where(seq > 0, hrecv[...].astype(F32), 0.0)
        for cb in range(4):
            mx[cb, 0:128, :] = wide[:, cb * 128 : cb * 128 + 128]

    def convolve(i, first_cb, n_cb):
        base = ROWS - PIECE * (i + 1)

        @pl.loop(0, 2 * n_cb)
        def _(n):
            cb = first_cb + n // 2
            row = pl.multiple_of(lax.rem(n, 2) * 64, 64)
            start = pl.multiple_of(base + row, 64)
            sums = [None] * 8
            for r in range(8):
                weights = [
                    jnp.broadcast_to(tapc[cb, 8 * m + r : 8 * m + r + 1, :], (8, 128)) for m in range(16)
                ]
                for w in range(-15, 8):
                    window = mx[cb, pl.ds(start + (128 + 8 * w - r), 8), :]
                    for m in range(16):
                        a = w + m
                        if 0 <= a < 8:
                            term = weights[m] * window
                            sums[a] = term if sums[a] is None else sums[a] + term
            lanes = pl.ds(pl.multiple_of(cb * 128, 128), 128)
            filtered = jnp.concatenate(sums, axis=0)
            query = acc[0, pl.ds(start, 64), lanes]
            gbuf[i, pl.ds(row, 64), lanes] = (query * filtered).astype(BF16)

    def exchange(i):
        return remote(
            gbuf.at[i, :, pl.ds(0, CH)], gbuf.at[i, :, pl.ds(CH, CH)], g_send.at[i], g_got.at[i], peer
        )

    def out_project(i):
        exchange(i).wait_recv()

        @pl.loop(0, RING)
        def _(d):
            pbuf[i, d] = jnp.dot(gbuf[i], wo[d], preferred_element_type=F32)

    def sum_right(i, d):
        return remote(sr.at[i, d - 1], rr.at[i, d - 1], rr_send.at[i, d - 1], rr_got.at[i, d - 1], right)

    def sum_left(i, d):
        return remote(sl.at[i, d - 1], rl.at[i, d - 1], rl_send.at[i, d - 1], rl_got.at[i, d - 1], left)

    def reduce_round(i, j):
        top_right = 4 if i % 2 == 0 else 3
        top_left = 7 - top_right
        d = top_right - j
        if d > 0:
            value = pbuf[i, d]
            if j > 0:
                sum_right(i, d + 1).wait_recv()
                value = value + rr[i, d].astype(F32)
            sr[i, d - 1] = value.astype(BF16)
            sum_right(i, d).start()
        d = top_left - j
        if d > 0:
            value = pbuf[i, RING - d]
            if j > 0:
                sum_left(i, d + 1).wait_recv()
                value = value + rl[i, d].astype(F32)
            sl[i, d - 1] = value.astype(BF16)
            sum_left(i, d).start()
        if j == 4:
            sum_right(i, 1).wait_recv()
            sum_left(i, 1).wait_recv()
            value = pbuf[i, 0] + rr[i, 0].astype(F32) + rl[i, 0].astype(F32)
            base = ROWS - PIECE * (i + 1)
            out_ref[base : base + PIECE, :] = value.astype(BF16)

    open_half(0)
    for pair in range(1, 8):
        for q in range(2):
            w_copy(pair, q).start()
    for cb in range(4):
        tap_copy(cb).start()
    for d in range(RING):
        wo_copy(d).start()
        wo_remote(d).start()
    for pair in range(8):
        for q in range(2):
            gp[pair : pair + 1, q * BLK : (q + 1) * BLK] = gain_ref[:, pl.ds(start_of(slots[pair][q], BLK), BLK)]
    project(0, 0)
    arrivals(0, 1)
    open_half(1)
    project(0, 1)
    arrivals(0, 2)
    project(0, 2)
    project(0, 3)
    arrivals(1, 1)
    project(1, 0)
    project(1, 1)
    arrivals(0, 3)
    project(0, 4)
    project(0, 5)
    arrivals(1, 2)
    project(1, 2)
    project(1, 3)
    arrivals(0, 4)
    project(0, 6)
    for cb in range(4):
        tap_copy(cb).wait()
        tapc[cb, 0:1, :] += skip_ref[:, cb * 128 : (cb + 1) * 128]
    arrivals(1, 3)
    project(0, 7)
    close_half(0)
    halo().start()
    project(1, 4)
    project(1, 5)
    convolve(0, 0, 2)
    arrivals(1, 4)
    convolve(0, 2, 2)
    exchange(0).start()
    project(1, 6)
    project(1, 7)
    close_half(1)
    take_halo()
    for d in range(RING):
        wo_copy(d).wait()
        wo_remote(d).wait_recv()

    out_project(0)
    reduce_round(0, 0)
    for i in (1, 2, 3):
        convolve(i, 0, 2)
        reduce_round(i - 1, 1)
        if i > 1:
            reduce_round(i - 2, 3)
        convolve(i, 2, 2)
        exchange(i).start()
        reduce_round(i - 1, 2)
        if i > 1:
            reduce_round(i - 2, 4)
        out_project(i)
        reduce_round(i, 0)
    reduce_round(3, 1)
    reduce_round(2, 3)
    reduce_round(3, 2)
    reduce_round(2, 4)
    reduce_round(3, 3)
    reduce_round(3, 4)

    for h in range(2):
        for s in range(4):
            if s < 3 or h == 0:
                to_right(h, s).wait_send()
            if s < 3 or h == 1:
                to_left(h, s).wait_send()
        for s in range(5):
            to_peer(h, s).wait_send()
    for d in range(RING):
        wo_remote(d).wait_send()
    halo().wait_send()
    for i in range(4):
        exchange(i).wait_send()
        for d in range(1, 5):
            if d < 4 or i % 2 == 0:
                sum_right(i, d).wait_send()
            if d < 4 or i % 2 == 1:
                sum_left(i, d).wait_send()


def on_device(tokens, norm_gain, in_weight, filter_taps, conv_skip, out_weight):
    vmem = pl.BlockSpec(memory_space=pltpu.VMEM)
    hbm = pl.BlockSpec(memory_space=pl.ANY)
    dma = pltpu.SemaphoreType.DMA
    return pl.pallas_call(
        mixer_kernel,
        out_shape=jax.ShapeDtypeStruct((ROWS, BLK), BF16),
        in_specs=[vmem, vmem, hbm, hbm, vmem, hbm],
        out_specs=vmem,
        scratch_shapes=[
            pltpu.VMEM((2, 8, HALF, 2 * BLK), BF16),
            pltpu.VMEM((HALF, 2 * BLK), BF16),
            pltpu.VMEM((8, 3, 2 * BLK, CH), BF16),
            pltpu.VMEM((RING, 2 * CH, BLK), BF16),
            pltpu.VMEM((3, ROWS, CH), F32),
            pltpu.VMEM((2, HALF, 128), F32),
            pltpu.VMEM((4, ROWS + 128, 128), F32),
            pltpu.VMEM((4, TAPS, 128), F32),
            pltpu.VMEM((8, 2 * BLK), F32),
            pltpu.VMEM((4, PIECE, 2 * CH), BF16),
            pltpu.VMEM((HALF, CH), BF16),
            pltpu.VMEM((128, CH), BF16),
            pltpu.VMEM((4, RING, PIECE, BLK), F32),
            pltpu.VMEM((4, 4, PIECE, BLK), BF16),
            pltpu.VMEM((4, 4, PIECE, BLK), BF16),
            pltpu.VMEM((4, 4, PIECE, BLK), BF16),
            pltpu.VMEM((4, 4, PIECE, BLK), BF16),
            dma((2, 4)), dma((2, 4)), dma((2, 5)), dma((2, 8, 2)), dma((8, 2)), dma((4,)),
            dma((8,)), dma((8,)), dma((8,)), dma((4,)), dma((4,)), dma((1,)), dma((1,)),
            dma((4, 4)), dma((4, 4)), dma((4, 4)), dma((4, 4)),
        ],
        compiler_params=pltpu.CompilerParams(
            collective_id=0, has_side_effects=True, vmem_limit_bytes=56 * 1024 * 1024
        ),
    )(tokens, norm_gain.reshape(1, -1), in_weight, filter_taps, conv_skip.reshape(1, -1), out_weight)


def solution(mesh):
    placed = (
        P("seq", ("trow", "tcol")),
        P(),
        P(None, None, ("trow", "tcol")),
        P(None, ("trow", "tcol")),
        P(("trow", "tcol")),
        P(("trow", "tcol"), None),
    )
    return jax.shard_map(
        on_device, mesh=mesh, in_specs=placed, out_specs=P("seq", ("trow", "tcol")), check_vma=False
    )
```

time: 222 us -> 97.8 us (0.44)
  the two profiles are of different devices: /device:TPU:1 before, /device:TPU:64 now
where the time goes in v1:
time: 97.8 us; the launch traced here: 97.6 us
  Pallas kernels  95.9 us (98%)
  local copies, waits for them, and re-layouts  1.67 us (2%)
    pallas_call x1, Pallas kernels, on_device(): pl.pallas_call(mixer_kernel, out_shape=jax.ShapeDtypeStruct((ROWS, BLK),...  95.9 us

profile of v1, /device:TPU:64, one launch (start us, length us, event | category | flops | bytes accessed | tf_op | source)
XLA Modules:
  0.0 97.6 jit_solution(15854597225914510229)
XLA Ops:
  0.0 95.9 %shard_map.64 = bf16[512,256]{1,0:T(8,128)(2,1)} custom-call(bf16[512,256]{1,0:T(8,128)(2,1)} %x_ref.1, f32[1,4096]{1,0:T(1,128)} %bitcast.2, bf16[3,4096,512]{2,1,0:T(8,128)(2,1)} %win.1, f32[128,512]{1,0:T(8,128)} %taps.1, f32[1,512]{1,0:T(1,128)} %bitcast.3, bf16[512,4096]{1,0:T(8,128)(2,1)} %wout.1), custom_call_target="tpu_custom_call" | custom-call | tf_op jit(solution)/shard_map/pallas_call | solution.py:353
  96.0 1.7 %copy.8 = bf16[512,256]{1,0:T(8,128)(2,1)} copy(bf16[512,256]{1,0:T(8,128)(2,1)} %shard_map.64) | data formatting | bytes 524288

commit v2 on v1

--- a/solution.py
+++ b/solution.py
@@ -21,7 +21,7 @@
 
 def mixer_kernel(
     x_ref, gain_ref, win, taps, skip_ref, wout, out_ref,
-    xg, xs, wv, wo, acc, sq, mx, tapc, gp, gbuf, hsend, hrecv, pbuf, rr, rl, sr, sl,
+    xg, xs, wv, wo, acc, sq, mx, sx, taps_v, tapc, gp, gbuf, hsend, hrecv, rr, rl, sr, sl,
     right_sem, left_sem, peer_sem, got, w_sem, tap_sem, wo_sem, wo_send, wo_got,
     g_send, g_got, h_send, h_got, rr_send, rl_send, rr_got, rl_got,
 ):
@@ -56,7 +56,7 @@
         )
 
     def tap_copy(cb):
-        return pltpu.make_async_copy(taps.at[:, pl.ds(cb * 128, 128)], tapc.at[cb], tap_sem.at[cb])
+        return pltpu.make_async_copy(taps.at[:, pl.ds(cb * 128, 128)], taps_v.at[cb], tap_sem.at[cb])
 
     def wo_copy(d):
         return pltpu.make_async_copy(
@@ -86,44 +86,48 @@
 
     rows_of = (pl.ds(HALF, HALF), pl.ds(0, HALF))
 
-    def slot(h, pair, q):
-        return xg.at[h, pair, :, pl.ds(q * BLK, BLK)]
-
-    def to_right(h, s):
-        src = x_ref.at[rows_of[h]] if s == 0 else slot(h, 2 * s - 1, 0)
-        dst_pair, dst_q = (2 * s + 1, 0) if s < 3 else (7, 0)
-        return remote(src, slot(h, dst_pair, dst_q), right_sem.at[h, s], got.at[h, dst_pair, dst_q], right)
-
-    def to_left(h, s):
-        src = x_ref.at[rows_of[h]] if s == 0 else slot(h, 2 * s - 1, 1)
-        dst_pair, dst_q = (2 * s + 1, 1) if s < 3 else (7, 0)
-        return remote(src, slot(h, dst_pair, dst_q), left_sem.at[h, s], got.at[h, dst_pair, dst_q], left)
-
-    def to_peer(h, s):
+    def quarter(u):
+        return pl.ds(ROWS - PIECE * (u + 1), PIECE)
+
+    def slots_of(u, pair, first, count):
+        rows = pl.ds(PIECE * (1 - u % 2), PIECE)
+        return xg.at[u // 2, pair, rows, pl.ds(first * BLK, count * BLK)]
+
+    def last_right(u):
+        return u % 2 == 0
+
+    def to_right(u, s):
+        src = x_ref.at[quarter(u)] if s == 0 else slots_of(u, 2 * s - 1, 0, 1)
+        pair = 2 * s + 1
+        return remote(src, slots_of(u, pair, 0, 1), right_sem.at[u, s], got.at[u, pair, 0], right)
+
+    def to_left(u, s):
+        src = x_ref.at[quarter(u)] if s == 0 else slots_of(u, 2 * s - 1, 1, 1)
+        pair, q = 2 * s + 1, (1 if s < 3 else 0)
+        return remote(src, slots_of(u, pair, q, 1), left_sem.at[u, s], got.at[u, pair, q], left)
+
+    def to_peer(u, s):
         if s == 0:
-            return remote(x_ref.at[rows_of[h]], slot(h, 0, 1), peer_sem.at[h, 0], got.at[h, 0, 1], peer)
+            return remote(x_ref.at[quarter(u)], slots_of(u, 0, 1, 1), peer_sem.at[u, 0], got.at[u, 0, 1], peer)
         if s == 4:
-            return remote(slot(h, 7, 0), slot(h, 7, 1), peer_sem.at[h, 4], got.at[h, 7, 1], peer)
-        return remote(xg.at[h, 2 * s - 1], xg.at[h, 2 * s], peer_sem.at[h, s], got.at[h, 2 * s, 0], peer)
-
-    def open_half(h):
-        to_right(h, 0).start()
-        to_left(h, 0).start()
-        to_peer(h, 0).start()
-
-    def arrivals(h, s):
+            return remote(slots_of(u, 7, 0, 1), slots_of(u, 7, 1, 1), peer_sem.at[u, 4], got.at[u, 7, 1], peer)
+        return remote(
+            slots_of(u, 2 * s - 1, 0, 2), slots_of(u, 2 * s, 0, 2), peer_sem.at[u, s], got.at[u, 2 * s, 0], peer
+        )
+
+    def arrivals(u, s):
         if s < 4:
-            to_right(h, s - 1).wait_recv()
-            if s < 3 or h == 0:
-                to_right(h, s).start()
-            to_left(h, s - 1).wait_recv()
-            if s < 3 or h == 1:
-                to_left(h, s).start()
-        elif h == 0:
-            to_right(h, 3).wait_recv()
+            to_right(u, s - 1).wait_recv()
+            if s < 3 or last_right(u):
+                to_right(u, s).start()
+            to_left(u, s - 1).wait_recv()
+            if s < 3 or not last_right(u):
+                to_left(u, s).start()
+        elif last_right(u):
+            to_right(u, 3).wait_recv()
         else:
-            to_left(h, 3).wait_recv()
-        to_peer(h, s).start()
+            to_left(u, 3).wait_recv()
+        to_peer(u, s).start()
 
     def project(h, pair):
         if h == 0:
@@ -131,11 +135,9 @@
             w_copy(pair, 1).wait()
         if pair == 0:
             xg[h, 0, :, 0:BLK] = x_ref[rows_of[h]]
-            to_peer(h, 0).wait_recv()
-        elif pair == 7:
-            to_peer(h, 4).wait_recv()
-        elif pair % 2 == 0:
-            to_peer(h, pair // 2).wait_recv()
+        if pair == 7 or pair % 2 == 0:
+            for u in (2 * h, 2 * h + 1):
+                to_peer(u, (pair + 1) // 2).wait_recv()
 
         @pl.loop(0, HALF // 32)
         def _(n):
@@ -185,42 +187,76 @@
         for cb in range(4):
             mx[cb, 0:128, :] = wide[:, cb * 128 : cb * 128 + 128]
 
+    def split_taps(cb):
+        tile = [taps_v[cb, 8 * m : 8 * m + 8, :] for m in range(16)]
+        for k in range(4):
+            even = [tile[4 * k], tile[4 * k + 2]]
+            odd = [tile[4 * k + 1], tile[4 * k + 3]]
+            both = [even[0] + odd[0], even[1] + odd[1]]
+            for p, (low, high) in enumerate((even, odd, both)):
+                for f, value in enumerate((low, high, low + high)):
+                    tapc[cb, 3 * p + f, 8 * k : 8 * k + 8, :] = value
+
     def convolve(i, first_cb, n_cb):
         base = ROWS - PIECE * (i + 1)
 
-        @pl.loop(0, 2 * n_cb)
-        def _(n):
-            cb = first_cb + n // 2
-            row = pl.multiple_of(lax.rem(n, 2) * 64, 64)
-            start = pl.multiple_of(base + row, 64)
-            sums = [None] * 8
-            for r in range(8):
-                weights = [
-                    jnp.broadcast_to(tapc[cb, 8 * m + r : 8 * m + r + 1, :], (8, 128)) for m in range(16)
-                ]
-                for w in range(-15, 8):
-                    window = mx[cb, pl.ds(start + (128 + 8 * w - r), 8), :]
-                    for m in range(16):
-                        a = w + m
-                        if 0 <= a < 8:
-                            term = weights[m] * window
-                            sums[a] = term if sums[a] is None else sums[a] + term
+        @pl.loop(first_cb, first_cb + n_cb)
+        def _(cb):
+            for t in range(31):
+                here = mx[cb, pl.ds(base + 8 * t, 8), :]
+                if t < 31:
+                    sx[1, 8 * t : 8 * t + 8, :] = here + mx[cb, pl.ds(base + 8 * t + 8, 8), :]
+                if t < 30:
+                    sx[0, 8 * t : 8 * t + 8, :] = here + mx[cb, pl.ds(base + 8 * t + 16, 8), :]
+            for t in range(29):
+                sx[2, 8 * t : 8 * t + 8, :] = sx[1, 8 * t : 8 * t + 8, :] + sx[1, 8 * t + 16 : 8 * t + 24, :]
+
+            def phase(p, with_before):
+                begin = -1 if with_before else 0
+                low = {c: None for c in range(begin, 4)}
+                high = {c: None for c in range(-1, 4)}
+                both = {c: None for c in range(begin, 4)}
+                for r in range(8):
+                    for f, sums in enumerate((low, high, both)):
+                        weights = [
+                            jnp.broadcast_to(tapc[cb, 3 * p + f, 8 * k + r : 8 * k + r + 1, :], (8, 128))
+                            for k in range(4)
+                        ]
+                        offset = (p if p < 2 else 0) + (2 if f == 1 else 0)
+                        for n in range(min(sums) - 3, 4):
+                            first = 128 + 8 * (4 * n + offset) - r
+                            if p < 2:
+                                window = mx[cb, pl.ds(base + first, 8), :] if f < 2 else sx[0, first : first + 8, :]
+                            else:
+                                window = sx[1, first : first + 8, :] if f < 2 else sx[2, first : first + 8, :]
+                            for k in range(4):
+                                if n + k in sums:
+                                    term = weights[k] * window
+                                    sums[n + k] = term if sums[n + k] is None else sums[n + k] + term
+                tiles = {}
+                for c in range(begin, 4):
+                    if c >= 0:
+                        tiles[2 * c] = low[c] + high[c - 1]
+                    tiles[2 * c + 1] = both[c] - low[c] - high[c]
+                return tiles
+
+            even = phase(0, False)
+            odd = phase(1, True)
+            both = phase(2, False)
             lanes = pl.ds(pl.multiple_of(cb * 128, 128), 128)
-            filtered = jnp.concatenate(sums, axis=0)
-            query = acc[0, pl.ds(start, 64), lanes]
-            gbuf[i, pl.ds(row, 64), lanes] = (query * filtered).astype(BF16)
+            for b in range(0, 8):
+                pair_of = (even[b] + odd[b - 1], both[b] - even[b] - odd[b])
+                filtered = jnp.concatenate(pair_of, axis=0)
+                query = acc[0, base + 16 * b : base + 16 * b + 16, lanes]
+                gbuf[i, 16 * b : 16 * b + 16, lanes] = (query * filtered).astype(BF16)
 
     def exchange(i):
         return remote(
             gbuf.at[i, :, pl.ds(0, CH)], gbuf.at[i, :, pl.ds(CH, CH)], g_send.at[i], g_got.at[i], peer
         )
 
-    def out_project(i):
-        exchange(i).wait_recv()
-
-        @pl.loop(0, RING)
-        def _(d):
-            pbuf[i, d] = jnp.dot(gbuf[i], wo[d], preferred_element_type=F32)
+    def share(i, d):
+        return jnp.dot(gbuf[i], wo[d], preferred_element_type=F32)
 
     def sum_right(i, d):
         return remote(sr.at[i, d - 1], rr.at[i, d - 1], rr_send.at[i, d - 1], rr_got.at[i, d - 1], right)
@@ -231,9 +267,11 @@
     def reduce_round(i, j):
         top_right = 4 if i % 2 == 0 else 3
         top_left = 7 - top_right
+        if j == 0:
+            exchange(i).wait_recv()
         d = top_right - j
         if d > 0:
-            value = pbuf[i, d]
+            value = share(i, d)
             if j > 0:
                 sum_right(i, d + 1).wait_recv()
                 value = value + rr[i, d].astype(F32)
@@ -241,20 +279,24 @@
             sum_right(i, d).start()
         d = top_left - j
         if d > 0:
-            value = pbuf[i, RING - d]
+            value = share(i, RING - d)
             if j > 0:
                 sum_left(i, d + 1).wait_recv()
                 value = value + rl[i, d].astype(F32)
             sl[i, d - 1] = value.astype(BF16)
             sum_left(i, d).start()
         if j == 4:
+            value = share(i, 0)
             sum_right(i, 1).wait_recv()
             sum_left(i, 1).wait_recv()
-            value = pbuf[i, 0] + rr[i, 0].astype(F32) + rl[i, 0].astype(F32)
+            value = value + rr[i, 0].astype(F32) + rl[i, 0].astype(F32)
             base = ROWS - PIECE * (i + 1)
             out_ref[base : base + PIECE, :] = value.astype(BF16)
 
-    open_half(0)
+    for u in range(4):
+        to_right(u, 0).start()
+        to_left(u, 0).start()
+        to_peer(u, 0).start()
     for pair in range(1, 8):
         for q in range(2):
             w_copy(pair, q).start()
@@ -267,73 +309,63 @@
         for q in range(2):
             gp[pair : pair + 1, q * BLK : (q + 1) * BLK] = gain_ref[:, pl.ds(start_of(slots[pair][q], BLK), BLK)]
     project(0, 0)
-    arrivals(0, 1)
-    open_half(1)
-    project(0, 1)
-    arrivals(0, 2)
-    project(0, 2)
-    project(0, 3)
-    arrivals(1, 1)
-    project(1, 0)
-    project(1, 1)
-    arrivals(0, 3)
-    project(0, 4)
-    project(0, 5)
-    arrivals(1, 2)
-    project(1, 2)
-    project(1, 3)
-    arrivals(0, 4)
-    project(0, 6)
-    for cb in range(4):
-        tap_copy(cb).wait()
-        tapc[cb, 0:1, :] += skip_ref[:, cb * 128 : (cb + 1) * 128]
-    arrivals(1, 3)
-    project(0, 7)
-    close_half(0)
-    halo().start()
-    project(1, 4)
-    project(1, 5)
-    convolve(0, 0, 2)
-    arrivals(1, 4)
-    convolve(0, 2, 2)
+    for s in range(1, 5):
+        arrivals(0, s)
+        project(1, 2 * s - 2)
+        arrivals(1, s)
+        if s < 4:
+            project(0, 2 * s - 1)
+        arrivals(2, s)
+        project(0, 2 * s if s < 4 else 7)
+        if s == 4:
+            close_half(0)
+            halo().start()
+        arrivals(3, s)
+        if s < 4:
+            project(1, 2 * s - 1)
+        if s == 1:
+            for cb in range(4):
+                tap_copy(cb).wait()
+                taps_v[cb, 0:1, :] += skip_ref[:, cb * 128 : (cb + 1) * 128]
+                split_taps(cb)
+
+    convolve(0, 0, 4)
     exchange(0).start()
-    project(1, 6)
     project(1, 7)
     close_half(1)
     take_halo()
     for d in range(RING):
         wo_copy(d).wait()
         wo_remote(d).wait_recv()
-
-    out_project(0)
     reduce_round(0, 0)
-    for i in (1, 2, 3):
-        convolve(i, 0, 2)
-        reduce_round(i - 1, 1)
-        if i > 1:
-            reduce_round(i - 2, 3)
-        convolve(i, 2, 2)
-        exchange(i).start()
-        reduce_round(i - 1, 2)
-        if i > 1:
-            reduce_round(i - 2, 4)
-        out_project(i)
-        reduce_round(i, 0)
-    reduce_round(3, 1)
-    reduce_round(2, 3)
-    reduce_round(3, 2)
-    reduce_round(2, 4)
-    reduce_round(3, 3)
-    reduce_round(3, 4)
-
-    for h in range(2):
+    convolve(1, 0, 4)
+    exchange(1).start()
+    reduce_round(1, 0)
+    convolve(2, 0, 2)
+    reduce_round(0, 1)
+    convolve(2, 2, 2)
+    exchange(2).start()
+    reduce_round(2, 0)
+    convolve(3, 0, 2)
+    reduce_round(1, 1)
+    reduce_round(0, 2)
+    convolve(3, 2, 2)
+    exchange(3).start()
+    reduce_round(3, 0)
+    for i, j in (
+        (2, 1), (1, 2), (0, 3), (3, 1), (2, 2), (1, 3), (0, 4),
+        (3, 2), (2, 3), (1, 4), (3, 3), (2, 4), (3, 4),
+    ):
+        reduce_round(i, j)
+
+    for u in range(4):
         for s in range(4):
-            if s < 3 or h == 0:
-                to_right(h, s).wait_send()
-            if s < 3 or h == 1:
-                to_left(h, s).wait_send()
+            if s < 3 or last_right(u):
+                to_right(u, s).wait_send()
+            if s < 3 or not last_right(u):
+                to_left(u, s).wait_send()
         for s in range(5):
-            to_peer(h, s).wait_send()
+            to_peer(u, s).wait_send()
     for d in range(RING):
         wo_remote(d).wait_send()
     halo().wait_send()
@@ -363,17 +395,18 @@
             pltpu.VMEM((3, ROWS, CH), F32),
             pltpu.VMEM((2, HALF, 128), F32),
             pltpu.VMEM((4, ROWS + 128, 128), F32),
+            pltpu.VMEM((3, 256, 128), F32),
             pltpu.VMEM((4, TAPS, 128), F32),
+            pltpu.VMEM((4, 9, 32, 128), F32),
             pltpu.VMEM((8, 2 * BLK), F32),
             pltpu.VMEM((4, PIECE, 2 * CH), BF16),
             pltpu.VMEM((HALF, CH), BF16),
             pltpu.VMEM((128, CH), BF16),
-            pltpu.VMEM((4, RING, PIECE, BLK), F32),
             pltpu.VMEM((4, 4, PIECE, BLK), BF16),
             pltpu.VMEM((4, 4, PIECE, BLK), BF16),
             pltpu.VMEM((4, 4, PIECE, BLK), BF16),
             pltpu.VMEM((4, 4, PIECE, BLK), BF16),
-            dma((2, 4)), dma((2, 4)), dma((2, 5)), dma((2, 8, 2)), dma((8, 2)), dma((4,)),
+            dma((4, 4)), dma((4, 4)), dma((4, 5)), dma((4, 8, 2)), dma((8, 2)), dma((4,)),
             dma((8,)), dma((8,)), dma((8,)), dma((4,)), dma((4,)), dma((1,)), dma((1,)),
             dma((4, 4)), dma((4, 4)), dma((4, 4)), dma((4, 4)),
         ],

time: 97.8 us -> 77.7 us (0.79)
  the two profiles are of different devices: /device:TPU:64 before, /device:TPU:1 now
where the time goes in v2:
time: 77.7 us; the launch traced here: 77.6 us
  Pallas kernels  75.9 us (98%)
  local copies, waits for them, and re-layouts  1.67 us (2%)
    pallas_call x1, Pallas kernels, on_device(): pl.pallas_call(mixer_kernel, out_shape=jax.ShapeDtypeStruct((ROWS, BLK),...  75.9 us
    unnamed x1, local copies, waits for them, and re-layouts  1.67 us

profile of v2, /device:TPU:1, one launch (start us, length us, event | category | flops | bytes accessed | tf_op | source)
XLA Modules:
  0.0 77.6 jit_solution(13328495098223400733)
XLA Ops:
  0.0 75.9 %shard_map.64 = bf16[512,256]{1,0:T(8,128)(2,1)} custom-call(bf16[512,256]{1,0:T(8,128)(2,1)} %x_ref.1, f32[1,4096]{1,0:T(1,128)} %bitcast.2, bf16[3,4096,512]{2,1,0:T(8,128)(2,1)} %win.1, f32[128,512]{1,0:T(8,128)} %taps.1, f32[1,512]{1,0:T(1,128)} %bitcast.3, bf16[512,4096]{1,0:T(8,128)(2,1)} %wout.1), custom_call_target="tpu_custom_call" | custom-call | tf_op jit(solution)/shard_map/pallas_call | solution.py:385
  75.9 1.7 %copy.8 = bf16[512,256]{1,0:T(8,128)(2,1)} copy(bf16[512,256]{1,0:T(8,128)(2,1)} %shard_map.64) | data formatting | bytes 524288

commit v3 on v2

--- a/solution.py
+++ b/solution.py
@@ -21,9 +21,9 @@
 
 def mixer_kernel(
     x_ref, gain_ref, win, taps, skip_ref, wout, out_ref,
-    xg, xs, wv, wo, acc, sq, mx, sx, taps_v, tapc, gp, gbuf, hsend, hrecv, rr, rl, sr, sl,
+    xg, xs, wv, wo, acc, sq, mx, sx, taps_v, tapc, gp, gbuf, hsend, hrecv, rr, rl, sr, sl, gain_v, skip_v, result,
     right_sem, left_sem, peer_sem, got, w_sem, tap_sem, wo_sem, wo_send, wo_got,
-    g_send, g_got, h_send, h_got, rr_send, rl_send, rr_got, rl_got,
+    g_send, g_got, h_send, h_got, rr_send, rl_send, rr_got, rl_got, own_sem, small_sem, out_sem,
 ):
     seq = lax.axis_index("seq")
     n_seq = lax.axis_size("seq")
@@ -77,21 +77,31 @@
             wo_send.at[d], wo_got.at[d], peer,
         )
 
+    def quarter(u):
+        return pl.ds(ROWS - PIECE * (u + 1), PIECE)
+
+    def own_copy(u):
+        return pltpu.make_async_copy(x_ref.at[quarter(u)], xg.at[u, 0, 0], own_sem.at[u])
+
     barrier = pltpu.get_barrier_semaphore()
-    for to in (right, left, peer, after, before):
+    for to in (right, left, peer, before):
         pl.semaphore_signal(barrier, inc=1, device_id=to, device_id_type=MESH)
+    local_copies = [
+        pltpu.make_async_copy(gain_ref, gain_v, small_sem.at[0]),
+        pltpu.make_async_copy(skip_ref, skip_v, small_sem.at[1]),
+    ]
+    for copy in local_copies:
+        copy.start()
+    for u in range(4):
+        own_copy(u).start()
     for q in range(2):
         w_copy(0, q).start()
-    pl.semaphore_wait(barrier, 5)
+    pl.semaphore_wait(barrier, 4)
 
     rows_of = (pl.ds(HALF, HALF), pl.ds(0, HALF))
 
-    def quarter(u):
-        return pl.ds(ROWS - PIECE * (u + 1), PIECE)
-
     def slots_of(u, pair, first, count):
-        rows = pl.ds(PIECE * (1 - u % 2), PIECE)
-        return xg.at[u // 2, pair, rows, pl.ds(first * BLK, count * BLK)]
+        return xg.at[u, pair, first] if count == 1 else xg.at[u, pair]
 
     def last_right(u):
         return u % 2 == 0
@@ -134,7 +144,8 @@
             w_copy(pair, 0).wait()
             w_copy(pair, 1).wait()
         if pair == 0:
-            xg[h, 0, :, 0:BLK] = x_ref[rows_of[h]]
+            for u in (2 * h, 2 * h + 1):
+                own_copy(u).wait()
         if pair == 7 or pair % 2 == 0:
             for u in (2 * h, 2 * h + 1):
                 to_peer(u, (pair + 1) // 2).wait_recv()
@@ -142,10 +153,15 @@
         @pl.loop(0, HALF // 32)
         def _(n):
             rows = pl.ds(pl.multiple_of(n * 32, 32), 32)
-            wide = xg[h, pair, rows, :].astype(F32)
-            xs[rows, :] = (wide * gp[pair : pair + 1, :]).astype(BF16)
-            square = wide * wide
-            square = square[:, 0:128] + square[:, 128:256] + square[:, 256:384] + square[:, 384:512]
+            u = 2 * h + 1 - n // 4
+            inner = pl.ds(pl.multiple_of(lax.rem(n, 4) * 32, 32), 32)
+            square = None
+            for q in range(2):
+                wide = xg[u, pair, q, inner, :].astype(F32)
+                xs[rows, q * BLK : (q + 1) * BLK] = (wide * gp[pair : pair + 1, q * BLK : (q + 1) * BLK]).astype(BF16)
+                term = wide * wide
+                term = term[:, 0:128] + term[:, 128:256]
+                square = term if square is None else square + term
             if pair == 0:
                 sq[h, rows, :] = square
             else:
@@ -264,6 +280,9 @@
     def sum_left(i, d):
         return remote(sl.at[i, d - 1], rl.at[i, d - 1], rl_send.at[i, d - 1], rl_got.at[i, d - 1], left)
 
+    def out_copy(i):
+        return pltpu.make_async_copy(result.at[i], out_ref.at[quarter(i)], out_sem.at[i])
+
     def reduce_round(i, j):
         top_right = 4 if i % 2 == 0 else 3
         top_left = 7 - top_right
@@ -290,8 +309,8 @@
             sum_right(i, 1).wait_recv()
             sum_left(i, 1).wait_recv()
             value = value + rr[i, 0].astype(F32) + rl[i, 0].astype(F32)
-            base = ROWS - PIECE * (i + 1)
-            out_ref[base : base + PIECE, :] = value.astype(BF16)
+            result[i] = value.astype(BF16)
+            out_copy(i).start()
 
     for u in range(4):
         to_right(u, 0).start()
@@ -305,58 +324,84 @@
     for d in range(RING):
         wo_copy(d).start()
         wo_remote(d).start()
+    for copy in local_copies:
+        copy.wait()
     for pair in range(8):
         for q in range(2):
-            gp[pair : pair + 1, q * BLK : (q + 1) * BLK] = gain_ref[:, pl.ds(start_of(slots[pair][q], BLK), BLK)]
+            gp[pair : pair + 1, q * BLK : (q + 1) * BLK] = gain_v[:, pl.ds(start_of(slots[pair][q], BLK), BLK)]
     project(0, 0)
-    for s in range(1, 5):
-        arrivals(0, s)
-        project(1, 2 * s - 2)
-        arrivals(1, s)
-        if s < 4:
-            project(0, 2 * s - 1)
-        arrivals(2, s)
-        project(0, 2 * s if s < 4 else 7)
-        if s == 4:
-            close_half(0)
-            halo().start()
-        arrivals(3, s)
-        if s < 4:
-            project(1, 2 * s - 1)
-        if s == 1:
-            for cb in range(4):
-                tap_copy(cb).wait()
-                taps_v[cb, 0:1, :] += skip_ref[:, cb * 128 : (cb + 1) * 128]
-                split_taps(cb)
-
+    arrivals(0, 1)
+    project(1, 0)
+    arrivals(1, 1)
+    project(0, 1)
+    arrivals(2, 1)
+    project(0, 2)
+    arrivals(3, 1)
+    project(1, 1)
+    for cb in range(4):
+        tap_copy(cb).wait()
+        taps_v[cb, 0:1, :] += skip_v[:, cb * 128 : (cb + 1) * 128]
+        split_taps(cb)
+    arrivals(0, 2)
+    project(1, 2)
+    arrivals(1, 2)
+    project(0, 3)
+    arrivals(2, 2)
+    project(0, 4)
+    arrivals(3, 2)
+    project(1, 3)
+    arrivals(0, 3)
+    project(1, 4)
+    arrivals(1, 3)
+    project(0, 5)
+    arrivals(2, 3)
+    project(0, 6)
+    arrivals(3, 3)
+    project(1, 5)
+    arrivals(0, 4)
+    arrivals(1, 4)
+    project(1, 6)
+    project(0, 7)
+    arrivals(2, 4)
+    arrivals(3, 4)
+    close_half(0)
+    halo().start()
     convolve(0, 0, 4)
     exchange(0).start()
     project(1, 7)
     close_half(1)
-    take_halo()
     for d in range(RING):
         wo_copy(d).wait()
         wo_remote(d).wait_recv()
     reduce_round(0, 0)
     convolve(1, 0, 4)
     exchange(1).start()
+    convolve(2, 0, 2)
     reduce_round(1, 0)
-    convolve(2, 0, 2)
-    reduce_round(0, 1)
     convolve(2, 2, 2)
     exchange(2).start()
+    reduce_round(0, 1)
+    take_halo()
+    convolve(3, 0, 2)
     reduce_round(2, 0)
-    convolve(3, 0, 2)
-    reduce_round(1, 1)
-    reduce_round(0, 2)
     convolve(3, 2, 2)
     exchange(3).start()
+    reduce_round(1, 1)
     reduce_round(3, 0)
-    for i, j in (
-        (2, 1), (1, 2), (0, 3), (3, 1), (2, 2), (1, 3), (0, 4),
-        (3, 2), (2, 3), (1, 4), (3, 3), (2, 4), (3, 4),
-    ):
-        reduce_round(i, j)
+    reduce_round(0, 2)
+    reduce_round(2, 1)
+    reduce_round(1, 2)
+    reduce_round(3, 1)
+    reduce_round(0, 3)
+    reduce_round(2, 2)
+    reduce_round(1, 3)
+    reduce_round(3, 2)
+    reduce_round(0, 4)
+    reduce_round(2, 3)
+    reduce_round(1, 4)
+    reduce_round(3, 3)
+    reduce_round(2, 4)
+    reduce_round(3, 4)
 
     for u in range(4):
         for s in range(4):
@@ -370,6 +415,7 @@
         wo_remote(d).wait_send()
     halo().wait_send()
     for i in range(4):
+        out_copy(i).wait()
         exchange(i).wait_send()
         for d in range(1, 5):
             if d < 4 or i % 2 == 0:
@@ -379,16 +425,15 @@
 
 
 def on_device(tokens, norm_gain, in_weight, filter_taps, conv_skip, out_weight):
-    vmem = pl.BlockSpec(memory_space=pltpu.VMEM)
-    hbm = pl.BlockSpec(memory_space=pl.ANY)
+    hbm = pl.BlockSpec(memory_space=pltpu.MemorySpace.HBM)
     dma = pltpu.SemaphoreType.DMA
     return pl.pallas_call(
         mixer_kernel,
         out_shape=jax.ShapeDtypeStruct((ROWS, BLK), BF16),
-        in_specs=[vmem, vmem, hbm, hbm, vmem, hbm],
-        out_specs=vmem,
+        in_specs=[hbm] * 6,
+        out_specs=hbm,
         scratch_shapes=[
-            pltpu.VMEM((2, 8, HALF, 2 * BLK), BF16),
+            pltpu.VMEM((4, 8, 2, PIECE, BLK), BF16),
             pltpu.VMEM((HALF, 2 * BLK), BF16),
             pltpu.VMEM((8, 3, 2 * BLK, CH), BF16),
             pltpu.VMEM((RING, 2 * CH, BLK), BF16),
@@ -406,9 +451,12 @@
             pltpu.VMEM((4, 4, PIECE, BLK), BF16),
             pltpu.VMEM((4, 4, PIECE, BLK), BF16),
             pltpu.VMEM((4, 4, PIECE, BLK), BF16),
+            pltpu.VMEM((1, 16 * BLK), F32),
+            pltpu.VMEM((1, CH), F32),
+            pltpu.VMEM((4, PIECE, BLK), BF16),
             dma((4, 4)), dma((4, 4)), dma((4, 5)), dma((4, 8, 2)), dma((8, 2)), dma((4,)),
             dma((8,)), dma((8,)), dma((8,)), dma((4,)), dma((4,)), dma((1,)), dma((1,)),
-            dma((4, 4)), dma((4, 4)), dma((4, 4)), dma((4, 4)),
+            dma((4, 4)), dma((4, 4)), dma((4, 4)), dma((4, 4)), dma((4,)), dma((2,)), dma((4,)),
         ],
         compiler_params=pltpu.CompilerParams(
             collective_id=0, has_side_effects=True, vmem_limit_bytes=56 * 1024 * 1024

time: 77.7 us -> 68.5 us (0.88); the launches traced: 77.6 us -> 67.6 us
  Pallas kernels: 75.9 us -> 65.9 us
    pallas_call x1, Pallas kernels: 75.9 us -> 65.9 us  [on_device(): pl.pallas_call(mixer_kernel, out_shape=jax.ShapeDtypeStruct((ROWS, BLK),...]
where the time goes in v3:
time: 68.5 us; the launch traced here: 67.6 us
  Pallas kernels  65.9 us (96%)
  local copies, waits for them, and re-layouts  1.67 us (2%)
    pallas_call x1, Pallas kernels, on_device(): pl.pallas_call(mixer_kernel, out_shape=jax.ShapeDtypeStruct((ROWS, BLK),...  65.9 us
    unnamed x1, local copies, waits for them, and re-layouts  1.67 us

profile of v3, /device:TPU:1, one launch (start us, length us, event | category | flops | bytes accessed | tf_op | source)
XLA Modules:
  0.0 67.6 jit_solution(12880665305241374582)
XLA Ops:
  0.0 65.9 %shard_map.64 = bf16[512,256]{1,0:T(8,128)(2,1)} custom-call(bf16[512,256]{1,0:T(8,128)(2,1)} %x_ref.1, f32[1,4096]{1,0:T(1,128)} %bitcast.2, bf16[3,4096,512]{2,1,0:T(8,128)(2,1)} %win.1, f32[128,512]{1,0:T(8,128)} %taps.1, f32[1,512]{1,0:T(1,128)} %bitcast.3, bf16[512,4096]{1,0:T(8,128)(2,1)} %wout.1), custom_call_target="tpu_custom_call" | custom-call | tf_op jit(solution)/shard_map/pallas_call | solution.py:430
  65.9 1.7 %copy.8 = bf16[512,256]{1,0:T(8,128)(2,1)} copy(bf16[512,256]{1,0:T(8,128)(2,1)} %shard_map.64) | data formatting | bytes 524288

commit v4 on v3

--- a/solution.py
+++ b/solution.py
@@ -274,74 +274,85 @@
     def share(i, d):
         return jnp.dot(gbuf[i], wo[d], preferred_element_type=F32)
 
-    def sum_right(i, d):
-        return remote(sr.at[i, d - 1], rr.at[i, d - 1], rr_send.at[i, d - 1], rr_got.at[i, d - 1], right)
-
-    def sum_left(i, d):
-        return remote(sl.at[i, d - 1], rl.at[i, d - 1], rl_send.at[i, d - 1], rl_got.at[i, d - 1], left)
+    def parts(i):
+        return 2 if i > 1 else 1
+
+    def sum_copy(i, d, part, sends, lands, send_sem, got_sem, to):
+        size = PIECE // parts(i)
+        rows = pl.ds(part * size, size)
+        return remote(
+            sends.at[i, d - 1, rows], lands.at[i, d - 1, rows], send_sem.at[i, d - 1, part], got_sem.at[i, d - 1, part], to
+        )
+
+    def sum_right(i, d, part):
+        return sum_copy(i, d, part, sr, rr, rr_send, rr_got, right)
+
+    def sum_left(i, d, part):
+        return sum_copy(i, d, part, sl, rl, rl_send, rl_got, left)
 
     def out_copy(i):
         return pltpu.make_async_copy(result.at[i], out_ref.at[quarter(i)], out_sem.at[i])
 
     def reduce_round(i, j):
         top_right = 4 if i % 2 == 0 else 3
-        top_left = 7 - top_right
         if j == 0:
             exchange(i).wait_recv()
-        d = top_right - j
-        if d > 0:
-            value = share(i, d)
-            if j > 0:
-                sum_right(i, d + 1).wait_recv()
-                value = value + rr[i, d].astype(F32)
-            sr[i, d - 1] = value.astype(BF16)
-            sum_right(i, d).start()
-        d = top_left - j
-        if d > 0:
-            value = share(i, RING - d)
-            if j > 0:
-                sum_left(i, d + 1).wait_recv()
-                value = value + rl[i, d].astype(F32)
-            sl[i, d - 1] = value.astype(BF16)
-            sum_left(i, d).start()
+        moves = []
+        for top, side, sends, lands, copy in (
+            (top_right, 1, sr, rr, sum_right), (7 - top_right, -1, sl, rl, sum_left)
+        ):
+            if top - j > 0:
+                moves.append((top - j, share(i, side * (top - j) % RING), sends, lands, copy))
         if j == 4:
             value = share(i, 0)
-            sum_right(i, 1).wait_recv()
-            sum_left(i, 1).wait_recv()
-            value = value + rr[i, 0].astype(F32) + rl[i, 0].astype(F32)
-            result[i] = value.astype(BF16)
+        size = PIECE // parts(i)
+        for part in range(parts(i)):
+            first, last = part * size, (part + 1) * size
+            for d, own, sends, lands, copy in moves:
+                total = own[first:last]
+                if j > 0:
+                    copy(i, d + 1, part).wait_recv()
+                    total = total + lands[i, d, first:last].astype(F32)
+                sends[i, d - 1, first:last] = total.astype(BF16)
+                copy(i, d, part).start()
+            if j == 4:
+                sum_right(i, 1, part).wait_recv()
+                sum_left(i, 1, part).wait_recv()
+                total = value[first:last] + rr[i, 0, first:last].astype(F32) + rl[i, 0, first:last].astype(F32)
+                result[i, first:last] = total.astype(BF16)
+        if j == 4:
             out_copy(i).start()
 
     for u in range(4):
         to_right(u, 0).start()
         to_left(u, 0).start()
         to_peer(u, 0).start()
+    for cb in range(4):
+        tap_copy(cb).start()
     for pair in range(1, 8):
         for q in range(2):
             w_copy(pair, q).start()
-    for cb in range(4):
-        tap_copy(cb).start()
-    for d in range(RING):
-        wo_copy(d).start()
-        wo_remote(d).start()
     for copy in local_copies:
         copy.wait()
     for pair in range(8):
         for q in range(2):
             gp[pair : pair + 1, q * BLK : (q + 1) * BLK] = gain_v[:, pl.ds(start_of(slots[pair][q], BLK), BLK)]
     project(0, 0)
+    project(1, 0)
+    for cb in range(4):
+        tap_copy(cb).wait()
+        taps_v[cb, 0:1, :] += skip_v[:, cb * 128 : (cb + 1) * 128]
+        split_taps(cb)
     arrivals(0, 1)
-    project(1, 0)
     arrivals(1, 1)
     project(0, 1)
     arrivals(2, 1)
     project(0, 2)
     arrivals(3, 1)
     project(1, 1)
-    for cb in range(4):
-        tap_copy(cb).wait()
-        taps_v[cb, 0:1, :] += skip_v[:, cb * 128 : (cb + 1) * 128]
-        split_taps(cb)
+    for d in range(RING):
+        wo_copy(d).start()
+        wo_remote(d).start()
     arrivals(0, 2)
     project(1, 2)
     arrivals(1, 2)
@@ -369,11 +380,11 @@
     convolve(0, 0, 4)
     exchange(0).start()
     project(1, 7)
-    close_half(1)
     for d in range(RING):
         wo_copy(d).wait()
         wo_remote(d).wait_recv()
     reduce_round(0, 0)
+    close_half(1)
     convolve(1, 0, 4)
     exchange(1).start()
     convolve(2, 0, 2)
@@ -418,10 +429,11 @@
         out_copy(i).wait()
         exchange(i).wait_send()
         for d in range(1, 5):
-            if d < 4 or i % 2 == 0:
-                sum_right(i, d).wait_send()
-            if d < 4 or i % 2 == 1:
-                sum_left(i, d).wait_send()
+            for part in range(parts(i)):
+                if d < 4 or i % 2 == 0:
+                    sum_right(i, d, part).wait_send()
+                if d < 4 or i % 2 == 1:
+                    sum_left(i, d, part).wait_send()
 
 
 def on_device(tokens, norm_gain, in_weight, filter_taps, conv_skip, out_weight):
@@ -456,7 +468,7 @@
             pltpu.VMEM((4, PIECE, BLK), BF16),
             dma((4, 4)), dma((4, 4)), dma((4, 5)), dma((4, 8, 2)), dma((8, 2)), dma((4,)),
             dma((8,)), dma((8,)), dma((8,)), dma((4,)), dma((4,)), dma((1,)), dma((1,)),
-            dma((4, 4)), dma((4, 4)), dma((4, 4)), dma((4, 4)), dma((4,)), dma((2,)), dma((4,)),
+            dma((4, 4, 2)), dma((4, 4, 2)), dma((4, 4, 2)), dma((4, 4, 2)), dma((4,)), dma((2,)), dma((4,)),
         ],
         compiler_params=pltpu.CompilerParams(
             collective_id=0, has_side_effects=True, vmem_limit_bytes=56 * 1024 * 1024

time: 68.5 us -> 68.5 us (level)
  no operation moved by 1% of the time
where the time goes in v4:
time: 68.5 us; the launch traced here: 68.1 us
  Pallas kernels  66.4 us (97%)
  local copies, waits for them, and re-layouts  1.67 us (2%)
    pallas_call x1, Pallas kernels, on_device(): pl.pallas_call(mixer_kernel, out_shape=jax.ShapeDtypeStruct((ROWS, BLK),...  66.4 us
    unnamed x1, local copies, waits for them, and re-layouts  1.67 us

profile of v4, /device:TPU:1, one launch (start us, length us, event | category | flops | bytes accessed | tf_op | source)
XLA Modules:
  0.0 68.1 jit_solution(9456195520033802661)
XLA Ops:
  0.0 66.4 %shard_map.64 = bf16[512,256]{1,0:T(8,128)(2,1)} custom-call(bf16[512,256]{1,0:T(8,128)(2,1)} %x_ref.1, f32[1,4096]{1,0:T(1,128)} %bitcast.2, bf16[3,4096,512]{2,1,0:T(8,128)(2,1)} %win.1, f32[128,512]{1,0:T(8,128)} %taps.1, f32[1,512]{1,0:T(1,128)} %bitcast.3, bf16[512,4096]{1,0:T(8,128)(2,1)} %wout.1), custom_call_target="tpu_custom_call" | custom-call | tf_op jit(solution)/shard_map/pallas_call | solution.py:442
  66.4 1.7 %copy.8 = bf16[512,256]{1,0:T(8,128)(2,1)} copy(bf16[512,256]{1,0:T(8,128)(2,1)} %shard_map.64) | data formatting | bytes 524288
